TPU v7x, 32 devices: a whole 2x2x4 slice. The times are simulated.
32 devices in a mesh: bins: 16 (over z, y, x), params: 2 (over core).
Axes of the slice: x: 2, y: 2, z: 4, core: 2. Of those that a mesh axis runs over, the one named last changes fastest.
Arguments:
- event_bins: int32 [49152], P('bins'), may hold values from 0 to 16383, as said below
- event_weights: bfloat16 [49152, 3072], P('bins', 'params'), may hold values from -6 to 6
- nominal: bfloat16 [49152], P('bins'), may hold values from 0.5 to 2
- background: float32 [16384], P('bins'), may hold values from 1 to 10
- observed: float32 [16384], P('bins'), may hold values from 1 to 100
Outputs:
- hessian: float32 [3072, 3072], P(('params', 'bins'))
Inputs may be any that keep to these rules, and one draw needn't show every extreme that they name: `event_bins`: each index of bins holds 3072 consecutive events in ascending bin order. The owner of bin b is b // 1024; each owner's bins receive from one index of bins between 96 and 288 of its events, and in every draw every index of bins has some owner that receives exactly 288 of its events.
All inputs are finite; a program needn't handle non-finite values.
Results may differ from a plain program's by a relative error of at most 0.0016.
Values may be sent and summed in bfloat16 or wider, within the bound.
A program may use at most 128 MiB of HBM per device.

v0:
```python
import math

import jax
import jax.numpy as jnp
from jax import lax
from jax.sharding import PartitionSpec as P


def from_behind(value, axis, steps):
    count = lax.axis_size(axis)
    pairs = [(source, (source + steps) % count) for source in range(count)]
    return lax.ppermute(value, axis, pairs)


def body(event_bins, event_weights, nominal, background, observed):
    owners = lax.axis_size("bins")
    groups_count = lax.axis_size("params")
    events = event_bins.shape[0]
    width_g = event_weights.shape[1]
    bins_dev = background.shape[0]
    capacity = 3 * events // (2 * owners)
    destination = event_bins // bins_dev
    targets = jnp.arange(owners, dtype=jnp.int32)
    starts = jnp.sum((destination[None, :] < targets[:, None]).astype(jnp.int32), axis=1)
    counts = jnp.sum((destination[None, :] == targets[:, None]).astype(jnp.int32), axis=1)
    slot_ids = jnp.arange(capacity, dtype=jnp.int32)
    filled = slot_ids[None, :] < counts[:, None]
    row_index = jnp.where(filled, starts[:, None] + slot_ids[None, :], 0)
    send_rows = jnp.where(filled[:, :, None], event_weights[row_index], jnp.zeros((), jnp.bfloat16))
    send_nominal = jnp.where(filled, nominal[row_index], jnp.zeros((), jnp.bfloat16))
    send_local = jnp.where(filled, event_bins[row_index] - targets[:, None] * bins_dev, -1)
    got_rows, got_nominal = (
        lax.all_to_all(send_rows, "bins", split_axis=0, concat_axis=0, tiled=True),
        lax.all_to_all(send_nominal, "bins", split_axis=0, concat_axis=0, tiled=True),
    )
    got_local = lax.all_to_all(send_local, "bins", split_axis=0, concat_axis=0, tiled=True)
    total_rows = owners * capacity
    block_rows = math.gcd(total_rows, 512)
    blocks = total_rows // block_rows
    bin_ids = jnp.arange(bins_dev, dtype=jnp.int32)
    dims = (((0,), (0,)), ((), ()))

    def add_block(carry, stacked):
        rows_block, nominal_block, local_block = stacked
        one_hot = (local_block[:, None] == bin_ids[None, :]).astype(jnp.bfloat16)
        hist_part = lax.dot_general(one_hot, rows_block, dims, preferred_element_type=jnp.float32)
        nominal_part = lax.dot_general(
            one_hot, nominal_block, dims, preferred_element_type=jnp.float32
        )
        return ((carry[0] + hist_part, carry[1] + nominal_part), None)

    start_sums = (jnp.zeros((bins_dev, width_g), jnp.float32), jnp.zeros((bins_dev,), jnp.float32))
    stacked_in = (
        got_rows.reshape(blocks, block_rows, width_g),
        got_nominal.reshape(blocks, block_rows),
        got_local.reshape(blocks, block_rows),
    )
    (histogram, nominal_sum), _ = lax.scan(add_block, start_sums, stacked_in)
    templates = histogram.astype(jnp.bfloat16)
    yields = background + nominal_sum
    curvature = observed / (yields * yields)
    weighted = (curvature[:, None] * templates.astype(jnp.float32)).astype(jnp.bfloat16)
    half_groups = groups_count // 2
    pieces = [templates]
    for shift_by in range(1, half_groups + 1):
        pieces.append(from_behind(templates, "params", -shift_by))
    partners = jnp.concatenate(pieces, axis=1)
    summed = lax.psum_scatter(
        lax.dot_general(weighted, partners, dims, preferred_element_type=jnp.float32),
        "bins",
        scatter_dimension=0,
        tiled=True,
    )
    return summed * (1.0 / (bins_dev * owners))


def solution(mesh):
    in_specs = (P("bins"), P("bins", "params"), P("bins"), P("bins"), P("bins"))
    out_specs = P(("params", "bins"), None)
    return jax.shard_map(body, mesh=mesh, in_specs=in_specs, out_specs=out_specs, check_vma=False)
```

profile of v0, /device:TPU:0, one launch (start us, length us, event | category | flops | bytes accessed | tf_op | source)
XLA Modules:
  0.0 838.4 jit_solution(8410196777892006943)
XLA Ops:
  6.5 0.0 copy-start
  6.5 0.7 add_select_fusion
  7.3 0.2 convert_reduce_fusion.1
  7.4 0.1 compare_select_fusion
  7.5 0.1 reshape.200
  7.6 0.0 copy-done
  7.6 0.0 copy-start.2
  7.6 27.3 %gather_fusion.2 = bf16[4608]{0:T(1024)(128)(2,1)S(1)} fusion(bf16[3072]{0:T(1024)(128)(2,1)S(1)} %copy-done, s32[5120]{0:T(1024)S(1)} %pad_clamp_fusion), kind=kCustom, calls=%fused_computation.2 | custom fusion | bytes 36864 | tf_op jit(solution)/shard_map/gather | solution.py:30
  34.9 0.1 gather.17
  35.0 0.1 fusion.16
  35.1 0.5 broadcast.195
  35.6 0.7 reduce.2
  36.3 0.7 reshape.232
  36.9 8.3 all-to-all-start.2
  45.3 0.0 copy-done.2
  45.3 24.1 %gather_fusion = s32[4608]{0:T(1024)S(1)} fusion(s32[3072]{0:T(1024)S(1)} %copy-done.2, s32[5120]{0:T(1024)S(1)} %pad_clamp_fusion), kind=kCustom, calls=%fused_computation | custom fusion | bytes 55296 | tf_op jit(solution)/shard_map/gather | solution.py:31
  69.4 0.1 gather.14
  69.5 0.1 subtract_select_fusion
  69.6 0.1 iota_compare_fusion.5
  69.6 33.2 %gather_fusion.1 = bf16[4608,1536]{1,0:T(8,128)(2,1)} fusion(bf16[3072,1536]{1,0:T(8,128)(2,1)} %param.8, s32[5120]{0:T(1024)S(1)} %pad_clamp_fusion), kind=kCustom, calls=%fused_computation.1 | custom fusion | bytes 28329984 | tf_op jit(solution)/shard_map/gather | solution.py:29
  102.8 0.6 copy.8
  103.5 0.0 all-to-all-done.2
  103.5 6.9 all-to-all-start
  110.4 10.6 %broadcast_select_fusion = bf16[16,288,1536]{2,1,0:T(8,128)(2,1)} fusion(bf16[16,288,1536]{2,1,0:T(8,128)(2,1)} %bitcast.20, pred[16,288]{1,0:T(8,128)(4,1)S(1)} %iota_compare_fusion.5), kind=kLoop, calls=%fused_computation.17 | loop fusion | flops 7077888 | bytes 28316160 | tf_op jit(solution)/shard_map/jit(_where)/select_n | solution.py:29
  121.0 0.0 all-to-all-done
  121.0 6.9 all-to-all-start.1
  128.0 0.2 reduce-scatter.2.cloned.1.call-start
  128.2 0.1 reshape.233
  128.3 0.1 reduce.1
  128.4 0.1 reshape.197
  128.5 0.1 reduce
  128.6 0.1 reshape.195
  128.6 262.5 %all-to-all-done.1 = bf16[16,288,1536]{2,1,0:T(8,128)(2,1)} async-done(((bf16[16,288,1536]{2,1,0:T(8,128)(2,1)}), bf16[16,288,1536]{2,1,0:T(8,128)(2,1)}, u32[]{:S(2)}, u32[]{:S(2)}) %all-to-all-start.1) | async-done | bytes 14155808 | tf_op jit(solution)/shard_map/all_to_all | solution.py:33
  391.2 73.2 %while.13 = (s32[]{:T(128)}, f32[1024,1536]{1,0:T(8,128)}, f32[1024]{0:T(1024)S(1)}, s32[9,512]{1,0:T(8,128)S(1)}, bf16[9,512,1536]{2,1,0:T(8,128)(2,1)}, /*index=5*/bf16[9,512]{1,0:T(8,128)(2,1)S(1)}, s32[]{:T(128)}, s32[]{:T(128)}) while((s32[]{:T(128)}, f32[1024,1536]{1,0:T(8,128)}, f32[1024]{0:T(1024)S(1)}, ...), condition=%wide.region_3.4_spmd.clone, body=%wide.region_2.3_spmd.clone.sunk | while | flops 1615857664 | bytes 14183016 | solution.py:58
  391.2 6.0 select_add_fusion.4
  397.1 0.5 fusion.25
  397.7 7.8 select_add_fusion.4
  405.5 0.5 fusion.25
  406.0 7.8 select_add_fusion.4
  413.8 0.5 fusion.25
  414.3 7.8 select_add_fusion.4
  422.2 0.5 fusion.25
  422.7 7.8 select_add_fusion.4
  430.5 0.5 fusion.25
  431.0 7.8 select_add_fusion.4
  438.9 0.5 fusion.25
  439.4 7.8 select_add_fusion.4
  447.2 0.5 fusion.25
  447.7 7.8 select_add_fusion.4
  455.5 0.5 fusion.25
  456.1 7.9 select_add_fusion.4
  463.9 0.5 fusion.25
  464.4 0.0 copy-start.3
  464.4 0.0 copy-start.4
  464.4 3.2 convert_element_type.18
  467.6 0.1 collective-permute-start
  467.7 0.0 copy-done.3
  467.7 0.0 copy-done.4
  467.7 5.6 collective-permute-done
  473.4 13.9 %fusion.11 = f32[1536,3072]{1,0:T(8,128)} fusion(bf16[1024,1536]{1,0:T(8,128)(2,1)S(1)} %collective-permute-done, bf16[1024,1536]{1,0:T(8,128)(2,1)S(1)} %convert_element_type.18, f32[1024]{0:T(1024)S(1)} %multiply_divide_fusion), kind=kOutput, calls=%fused_computation.18 | convolution fusion | flops 9680977920 | bytes 25169920 | tf_op jit(solution)/shard_map/dot_general | solution.py:69
  487.2 0.0 reduce-scatter.2.cloned.1.call-update
  487.2 341.9 %reduce-scatter.2.cloned.1.call-done = f32[96,3072]{1,0:T(8,128)} async-done(((f32[1536,3072]{1,0:T(8,128)}), f32[96,3072]{1,0:T(8,128)}) %reduce-scatter.2.cloned.1.call-update) | async-done | bytes 1179664 | tf_op jit(solution)/shard_map/reduce_scatter | solution.py:68
  829.1 2.4 broadcast_multiply_fusion
  831.5 0.0 copy-done.1
  (24 shorter events, 0.2 us)
Async XLA Ops:
  6.5 1.1 copy-start
  7.6 37.7 %copy-start.2 = (s32[3072]{0:T(1024)S(1)}, s32[3072]{0:T(1024)}, u32[]{:S(2)}) copy-start(s32[3072]{0:T(1024)} %param.7) | copy-start | bytes 36868
  36.9 66.5 %all-to-all-start.2 = ((bf16[16,2,144]{2,1,0:T(2,128)(2,1)}), bf16[16,2,144]{2,1,0:T(2,128)(2,1)S(1)}, u32[]{:S(2)}, u32[]{:S(2)}) async-start(bf16[16,2,144]{2,1,0:T(2,128)(2,1)} %reshape.232), calls=%async_computation.2 | async-start | bytes 32768 | tf_op jit(solution)/shard_map/all_to_all | solution.py:34
  103.5 17.5 %all-to-all-start = ((s32[16,1,288]{2,1,0:T(1,128)}), s32[16,1,288]{2,1,0:T(1,128)S(1)}, u32[]{:S(2)}, u32[]{:S(2)}) async-start(s32[16,1,288]{2,1,0:T(1,128)} %copy.8), calls=%async_computation | async-start | bytes 49152 | tf_op jit(solution)/shard_map/all_to_all | solution.py:36
  121.0 270.1 %all-to-all-start.1 = ((bf16[16,288,1536]{2,1,0:T(8,128)(2,1)}), bf16[16,288,1536]{2,1,0:T(8,128)(2,1)}, u32[]{:S(2)}, u32[]{:S(2)}) async-start(bf16[16,288,1536]{2,1,0:T(8,128)(2,1)} %broadcast_select_fusion), calls=%async_computation.1 | async-start | bytes 28311552 | tf_op jit(solution)/shard_map/all_to_all | solution.py:33
  128.0 701.2 %reduce-scatter.2.cloned.1.call-start = ((), (), s32[]{:S(2)}) async-start(), calls=%async_computation.4 | async-start | bytes 20054016 | tf_op jit(solution)/shard_map/reduce_scatter | solution.py:68
  464.4 3.3 copy-start.3
  464.4 3.3 copy-start.4
  467.6 5.7 collective-permute-start
  487.2 344.3 %copy-start.1 = (bf16[3072]{0:T(1024)(128)(2,1)S(1)}, bf16[3072]{0:T(1024)(128)(2,1)}, u32[]{:S(2)}) copy-start(bf16[3072]{0:T(1024)(128)(2,1)} %param.9) | copy-start | bytes 18436
Sparse Core Ops, SparseCore 0:
  487.4 341.7 reduce-scatter.1
where the time goes:
time: 839 us; the launch traced here: 838 us
  waiting for transfers between devices  610 us (73%)
  local copies, waits for them, and re-layouts  87 us (10%)
  matrix products  86.9 us (10%)
  starting transfers between devices  22.5 us (3%)
  other arithmetic  18.3 us (2%)
  between operations  13.6 us (2%)
    reduce_scatter x1, waiting for transfers between devices, body(): lax.psum_scatter(lax.dot_general(weighted, partners, dims, preferred_elem...  342 us
    all_to_all x1, waiting for transfers between devices, body(): lax.all_to_all(send_rows, 'bins', split_axis=0, concat_axis=0, tiled=True)  263 us
    dot_general x9, matrix products, add_block(): lax.dot_general(one_hot, rows_block, dims, preferred_element_type=jnp.flo...  68.7 us
    gather x1, local copies, waits for them, and re-layouts, body(): event_weights[row_index]  33.2 us
    gather x2, local copies, waits for them, and re-layouts, body(): nominal[row_index]  27.4 us
    gather x2, local copies, waits for them, and re-layouts, body(): event_bins[row_index] - targets[:, None] * bins_dev  24.2 us
  transfers between devices with their start and end apart: 5, of which 3 were waited for; matrix products, arithmetic and copies ran while one was open for 8% of the time, Pallas kernels for 0%

commit v1 on v0

v1 whole, which is shorter than its diff:
```python
import functools
import math

import jax
import jax.numpy as jnp
from jax import lax
from jax.experimental import pallas as pl
from jax.experimental.pallas import tpu as pltpu
from jax.sharding import PartitionSpec as P

ALIGN = 8


def from_behind(value, axis, steps):
    count = lax.axis_size(axis)
    pairs = [(source, (source + steps) % count) for source in range(count)]
    return lax.ppermute(value, axis, pairs)


def pack_kernel(owners, slot, first, width, starts_ref, rows_ref, out_ref, held, in_sems, out_sems):
    def fetch(o):
        start = pl.multiple_of(starts_ref[o] * ALIGN, ALIGN)
        return pltpu.make_async_copy(
            rows_ref.at[pl.ds(start, slot), pl.ds(first, width)], held.at[o], in_sems.at[o]
        )

    def store(o):
        return pltpu.make_async_copy(held.at[o], out_ref.at[o], out_sems.at[o])

    @pl.loop(0, owners)
    def _(o):
        fetch(o).start()

    @pl.loop(0, owners)
    def _(o):
        fetch(o).wait()
        store(o).start()

    @pl.loop(0, owners)
    def _(o):
        store(o).wait()


def pack(starts, rows, slot, first, width):
    owners = starts.shape[0]
    return pl.pallas_call(
        functools.partial(pack_kernel, owners, slot, first, width),
        out_shape=jax.ShapeDtypeStruct((owners, slot, width), rows.dtype),
        in_specs=[
            pl.BlockSpec(memory_space=pltpu.SMEM),
            pl.BlockSpec(memory_space=pl.ANY),
        ],
        out_specs=pl.BlockSpec(memory_space=pl.ANY),
        scratch_shapes=[
            pltpu.VMEM((owners, slot, width), rows.dtype),
            pltpu.SemaphoreType.DMA((owners,)),
            pltpu.SemaphoreType.DMA((owners,)),
        ],
        compiler_params=pltpu.CompilerParams(vmem_limit_bytes=32 << 20),
        cost_estimate=pl.CostEstimate(
            flops=0, bytes_accessed=4 * owners * slot * width, transcendentals=0
        ),
        name="pack",
    )(starts, rows)


def meta_kernel(bins_dev, starts_ref, table_ref, out_ref):
    owners, _, slot = out_ref.shape
    events = table_ref.shape[1]
    table = table_ref[...]

    @pl.loop(0, owners)
    def _(o):
        start = starts_ref[o] * ALIGN
        turned = pltpu.roll(table, lax.rem(events - start, events), axis=1)[:, :slot]
        bins = turned[0:1] - (o * bins_dev).astype(jnp.float32)
        inside = (bins >= 0) & (bins < bins_dev)
        out_ref[o, 0:1, :] = jnp.where(inside, bins, -1.0)
        out_ref[o, 1:2, :] = turned[1:2]


def pack_meta(starts, table, slot, bins_dev):
    owners = starts.shape[0]
    return pl.pallas_call(
        functools.partial(meta_kernel, bins_dev),
        out_shape=jax.ShapeDtypeStruct((owners, 2, slot), jnp.float32),
        in_specs=[
            pl.BlockSpec(memory_space=pltpu.SMEM),
            pl.BlockSpec(memory_space=pltpu.VMEM),
        ],
        out_specs=pl.BlockSpec(memory_space=pltpu.VMEM),
        name="pack_meta",
    )(starts, table)


def hist_kernel(chunk, tile, local_ref, rows_ref, out_ref, hot):
    bins, total = hot.shape

    @pl.when(pl.program_id(0) == 0)
    def _():
        ids = lax.broadcasted_iota(jnp.int32, (bins, chunk), 0)

        @pl.loop(0, total // chunk)
        def _(k):
            part = pl.ds(pl.multiple_of(k * chunk, chunk), chunk)
            hot[:, part] = (ids == local_ref[:, part]).astype(jnp.bfloat16)

    @pl.loop(0, bins // tile)
    def _(m):
        part = pl.ds(pl.multiple_of(m * tile, tile), tile)
        out_ref[part, :] = jnp.dot(
            hot[part, :], rows_ref[...], preferred_element_type=jnp.float32
        ).astype(out_ref.dtype)


def histogram_of(local, rows, bins, block, dtype):
    total, width = rows.shape
    return pl.pallas_call(
        functools.partial(hist_kernel, math.gcd(total, 128), math.gcd(bins, 256)),
        grid=(width // block,),
        out_shape=jax.ShapeDtypeStruct((bins, width), dtype),
        in_specs=[
            pl.BlockSpec((1, total), lambda j: (0, 0)),
            pl.BlockSpec((total, block), lambda j: (0, j)),
        ],
        out_specs=pl.BlockSpec((bins, block), lambda j: (0, j)),
        scratch_shapes=[pltpu.VMEM((bins, total), jnp.bfloat16)],
        compiler_params=pltpu.CompilerParams(
            vmem_limit_bytes=40 << 20, dimension_semantics=("arbitrary",)
        ),
        cost_estimate=pl.CostEstimate(
            flops=2 * bins * total * width, bytes_accessed=2 * total * width, transcendentals=0
        ),
        name="histogram",
    )(local, rows)


def body(event_bins, event_weights, nominal, background, observed):
    owners = lax.axis_size("bins")
    groups_count = lax.axis_size("params")
    events = event_bins.shape[0]
    width_g = event_weights.shape[1]
    bins_dev = background.shape[0]
    capacity = 3 * events // (2 * owners)
    slot = -(-capacity // ALIGN) * ALIGN + ALIGN
    chunks = 2 if width_g % 512 == 0 else 1
    width = width_g // chunks
    block = math.gcd(width, 256)

    destination = event_bins // bins_dev
    targets = jnp.arange(owners, dtype=jnp.int32)
    before = jnp.sum((destination[None, :] < targets[:, None]).astype(jnp.int32), axis=1)
    starts = jnp.minimum(before // ALIGN, (events - slot) // ALIGN)

    table = jnp.stack([event_bins.astype(jnp.float32), nominal.astype(jnp.float32)])
    table = jnp.concatenate([table, jnp.zeros((6, events), jnp.float32)], axis=0)
    meta = pack_meta(starts, table, slot, bins_dev)
    got_meta = lax.all_to_all(meta, "bins", split_axis=0, concat_axis=0, tiled=True)
    local = got_meta[:, 0].astype(jnp.int32).reshape(1, owners * slot)
    got_nominal = got_meta[:, 1].astype(jnp.bfloat16).reshape(owners * slot, 1)
    got_nominal = jnp.broadcast_to(got_nominal, (owners * slot, 128))
    nominal_sum = histogram_of(local, got_nominal, bins_dev, 128, jnp.float32)[:, 0]
    yields = background + nominal_sum
    curvature = observed / (yields * yields)

    parts = []
    for c in range(chunks):
        packed = pack(starts, event_weights, slot, c * width, width)
        got = lax.all_to_all(packed, "bins", split_axis=0, concat_axis=0, tiled=True)
        got = got.reshape(owners * slot, width)
        parts.append(histogram_of(local, got, bins_dev, block, jnp.bfloat16))
    templates = jnp.concatenate(parts, axis=1)
    weighted = (curvature[:, None] * templates.astype(jnp.float32)).astype(jnp.bfloat16)
    pieces = [templates]
    for shift_by in range(1, groups_count // 2 + 1):
        shifted = [from_behind(part, "params", -shift_by) for part in parts]
        pieces.append(jnp.concatenate(shifted, axis=1))
    partners = jnp.concatenate(pieces, axis=1)
    dims = (((0,), (0,)), ((), ()))
    full = lax.dot_general(weighted, partners, dims, preferred_element_type=jnp.float32)
    full = full.astype(jnp.bfloat16)
    shares = full.reshape(owners, width_g // owners, full.shape[1])
    got = lax.all_to_all(shares, "bins", split_axis=0, concat_axis=0, tiled=True)
    summed = jnp.sum(got.astype(jnp.float32), axis=0)
    return summed * (1.0 / (bins_dev * owners))


def solution(mesh):
    in_specs = (P("bins"), P("bins", "params"), P("bins"), P("bins"), P("bins"))
    out_specs = P(("params", "bins"), None)
    return jax.shard_map(body, mesh=mesh, in_specs=in_specs, out_specs=out_specs, check_vma=False)
```

time: 839 us -> 615 us (0.73)
  waiting for transfers between devices: 610 us -> 240 us
  blocking collectives: 0 us -> 239 us
  matrix products: 86.9 us -> 13.7 us
  local copies, waits for them, and re-layouts: 87 us -> 16.8 us
  Pallas kernels: 0 us -> 49.3 us
  starting transfers between devices: 22.5 us -> 49.9 us
  between operations: 13.6 us -> 0.22 us
  other arithmetic: 18.3 us -> 5.96 us
    reduce_scatter x1 -> x0, waiting for transfers between devices: 342 us -> none  [body(): lax.psum_scatter(lax.dot_general(weighted, partners, dims, preferred_elem...]
    all_to_all x0 -> x1, blocking collectives: none -> 239 us  [body(): lax.all_to_all(shares, 'bins', split_axis=0, concat_axis=0, tiled=True)]
    gather x5 -> x0, local copies, waits for them, and re-layouts: 84.7 us -> none  [the longest x1 33.2 us: body(): event_weights[row_index]]
    dot_general x18 -> x0, matrix products: 73 us -> none  [the longest x9 68.7 us: add_block(): lax.dot_general(one_hot, rows_block, dims, preferred_element_type=jnp.flo...]
    pallas_call x0 -> x6, Pallas kernels: none -> 49.3 us  [the longest x3 33.9 us: histogram_of(): pl.pallas_call(functools.partial(hist_kernel, math.gcd(total, 128), math....]
    all_to_all x3, starting transfers between devices: 22.2 us -> 49.7 us  [the longest x2 41.4 us: body(): lax.all_to_all(packed, 'bins', split_axis=0, concat_axis=0, tiled=True)]
    all_to_all x3, waiting for transfers between devices: 263 us -> 240 us  [the longest x2 240 us: body(): lax.all_to_all(packed, 'bins', split_axis=0, concat_axis=0, tiled=True)]
    unnamed x12 -> x16, local copies, waits for them, and re-layouts: 0.8 us -> 13.8 us
  transfers between devices with their start and end apart: 5 -> 5, of which waited for: 3 -> 2; matrix products, arithmetic and copies ran while one was open for 8% -> 0% of each run, Pallas kernels for 0% -> 7%
where the time goes in v1:
time: 615 us
  waiting for transfers between devices  240 us (39%)
  blocking collectives  239 us (39%)
  starting transfers between devices  49.9 us (8%)
  Pallas kernels  49.3 us (8%)
  local copies, waits for them, and re-layouts  16.8 us (3%)
  matrix products  13.7 us (2%)
    all_to_all x2, waiting for transfers between devices, body(): lax.all_to_all(packed, 'bins', split_axis=0, concat_axis=0, tiled=True)  240 us
    all_to_all x1, blocking collectives, body(): lax.all_to_all(shares, 'bins', split_axis=0, concat_axis=0, tiled=True)  239 us
    all_to_all x2, starting transfers between devices, body(): lax.all_to_all(packed, 'bins', split_axis=0, concat_axis=0, tiled=True)  41.4 us
    pallas_call x3, Pallas kernels, histogram_of(): pl.pallas_call(functools.partial(hist_kernel, math.gcd(total, 128), math....  33.9 us
    unnamed x16, local copies, waits for them, and re-layouts  13.8 us
    dot_general x1, matrix products, body(): lax.dot_general(weighted, partners, dims, preferred_element_type=jnp.floa...  13.7 us
  transfers between devices with their start and end apart: 5, of which 2 were waited for; matrix products, arithmetic and copies ran while one was open for 0% of the time, Pallas kernels for 7%

profile of v1, /device:TPU:0, one launch (start us, length us, event | category | flops | bytes accessed | tf_op | source)
XLA Modules:
  0.0 614.8 jit_solution(16515297478214311053)
XLA Ops:
  0.0 0.7 stack.12
  0.7 0.8 fusion.17
  1.5 0.1 convert_reduce_fusion.1
  1.6 0.5 fusion.15.starts_ref
  2.2 0.1 pad.8.clone
  2.2 0.7 maximum_maximum_fusion.table_ref
  3.0 3.4 pack_meta.1
  6.3 8.3 %all-to-all-start = ((f32[16,2,296]{2,1,0:T(2,128)}), f32[16,2,296]{2,1,0:T(2,128)S(1)}, u32[]{:S(2)}, u32[]{:S(2)}) async-start(f32[16,2,296]{2,1,0:T(2,128)} %pack_meta.1), calls=%async_computation | async-start | bytes 98304 | tf_op jit(solution)/shard_map/all_to_all | solution.py:158
  14.7 0.0 copy-start
  14.7 3.7 copy-done
  18.3 0.0 copy-start.4
  18.4 0.6 copy-done.4
  19.0 6.0 pack.3
  25.0 0.0 copy-start.3
  25.0 3.0 copy-done.3
  27.9 0.0 copy-start.5
  27.9 0.0 all-to-all-done
  27.9 7.0 %all-to-all-start.2 = ((bf16[16,296,768]{2,1,0:T(8,128)(2,1)}), bf16[16,296,768]{2,1,0:T(8,128)(2,1)}, u32[]{:S(2)}, u32[]{:S(2)}) async-start(bf16[16,296,768]{2,1,0:T(8,128)(2,1)} %copy-done.3), calls=%async_computation.2 | async-start | bytes 14548992 | tf_op jit(solution)/shard_map/all_to_all | solution.py:169
  34.9 0.0 copy-done.5
  34.9 0.0 copy-start.1
  34.9 3.7 copy-done.1
  38.6 6.0 pack.2
  44.6 0.0 copy-start.2
  44.6 2.9 copy-done.2
  47.5 122.3 %all-to-all-done.2 = bf16[16,296,768]{2,1,0:T(8,128)(2,1)} async-done(((bf16[16,296,768]{2,1,0:T(8,128)(2,1)}), bf16[16,296,768]{2,1,0:T(8,128)(2,1)}, u32[]{:S(2)}, u32[]{:S(2)}) %all-to-all-start.2) | async-done | bytes 7274528 | tf_op jit(solution)/shard_map/all_to_all | solution.py:169
  169.8 34.4 %all-to-all-start.1 = ((bf16[16,296,768]{2,1,0:T(8,128)(2,1)}), bf16[16,296,768]{2,1,0:T(8,128)(2,1)}, u32[]{:S(2)}, u32[]{:S(2)}) async-start(bf16[16,296,768]{2,1,0:T(8,128)(2,1)} %copy-done.2), calls=%async_computation.1 | async-start | bytes 14548992 | tf_op jit(solution)/shard_map/all_to_all | solution.py:169
  204.2 0.1 fusion.12
  204.3 0.1 convert_element_type.43.local_ref
  204.4 14.1 %histogram.5 = bf16[1024,768]{1,0:T(8,128)(2,1)S(1)} custom-call(s32[1,4736]{1,0:T(1,128)S(1)} %convert_element_type.43.local_ref, bf16[4736,768]{1,0:T(8,128)(2,1)} %bitcast.3.rows_ref), custom_call_target="tpu_custom_call" | custom-call | flops 7449083904 | bytes 7274496 | tf_op jit(solution)/shard_map/histogram/pallas_call | solution.py:118
  218.6 0.1 collective-permute-start.1
  218.7 117.7 %all-to-all-done.1 = bf16[16,296,768]{2,1,0:T(8,128)(2,1)} async-done(((bf16[16,296,768]{2,1,0:T(8,128)(2,1)}), bf16[16,296,768]{2,1,0:T(8,128)(2,1)}, u32[]{:S(2)}, u32[]{:S(2)}) %all-to-all-start.1) | async-done | bytes 7274528 | tf_op jit(solution)/shard_map/all_to_all | solution.py:169
  336.4 14.1 %histogram.4 = bf16[1024,768]{1,0:T(8,128)(2,1)S(1)} custom-call(s32[1,4736]{1,0:T(1,128)S(1)} %convert_element_type.43.local_ref, bf16[4736,768]{1,0:T(8,128)(2,1)} %bitcast.2.rows_ref), custom_call_target="tpu_custom_call" | custom-call | flops 7449083904 | bytes 7274496 | tf_op jit(solution)/shard_map/histogram/pallas_call | solution.py:118
  350.6 0.0 copy-start.6
  350.6 0.0 copy-start.7
  350.6 0.1 collective-permute-start
  350.7 0.1 fusion.11
  350.7 0.1 convert_element_type.44
  350.9 2.3 broadcast_in_dim.5.rows_ref
  353.2 5.6 histogram.3
  358.8 0.2 slice_reduce_fusion
  359.0 0.0 copy-done.6
  359.1 0.0 copy-done.7
  359.1 0.0 collective-permute-done.1
  359.1 0.0 collective-permute-done
  359.1 13.7 %convolution_convert_fusion = bf16[1536,3072]{1,0:T(8,128)(2,1)} fusion(bf16[1024,768]{1,0:T(8,128)(2,1)} %collective-permute-done.1, bf16[1024,768]{1,0:T(8,128)(2,1)} %collective-permute-done, bf16[1024,768]{1,0:T(8,128)(2,1)S(1)} %histogram.5, bf16[1024,768]{1,0:T(8,128)(2,1)S(1)} %histogram.4, f32[1024]{0:T(1024)S(1)} %multiply_divide_fusion), kind=kOutput, calls=%fused_computation.1 | convolution fusion | flops 9702998016 | bytes 15732736 | tf_op jit(solution)/shard_map/dot_general | solution.py:180
  372.8 239.0 %all_to_all.20 = bf16[16,96,3072]{2,1,0:T(8,128)(2,1)S(1)} all-to-all(bf16[16,96,3072]{2,1,0:T(8,128)(2,1)} %bitcast.5), channel_id=1, replica_groups=mesh['bins'=16,'params'=2] {'bins'}, dimensions={0} | all-to-all | bytes 18874368 | tf_op jit(solution)/shard_map/all_to_all | solution.py:183
  611.8 1.9 convert_reduce_fusion
  613.7 1.1 broadcast_multiply_fusion
  (2 shorter events, 0.0 us)
Async XLA Ops:
  6.3 21.6 %all-to-all-start = ((f32[16,2,296]{2,1,0:T(2,128)}), f32[16,2,296]{2,1,0:T(2,128)S(1)}, u32[]{:S(2)}, u32[]{:S(2)}) async-start(f32[16,2,296]{2,1,0:T(2,128)} %pack_meta.1), calls=%async_computation | async-start | bytes 98304 | tf_op jit(solution)/shard_map/all_to_all | solution.py:158
  14.7 3.7 copy-start
  18.3 0.6 copy-start.4
  25.0 3.0 copy-start.3
  27.9 7.0 %copy-start.5 = (s32[16]{0:T(128)S(1)}, s32[16]{0:T(128)}, u32[]{:S(2)}) copy-start(s32[16]{0:T(128)} %fusion.15.starts_ref) | copy-start | bytes 196
  27.9 141.9 %all-to-all-start.2 = ((bf16[16,296,768]{2,1,0:T(8,128)(2,1)}), bf16[16,296,768]{2,1,0:T(8,128)(2,1)}, u32[]{:S(2)}, u32[]{:S(2)}) async-start(bf16[16,296,768]{2,1,0:T(8,128)(2,1)} %copy-done.3), calls=%async_computation.2 | async-start | bytes 14548992 | tf_op jit(solution)/shard_map/all_to_all | solution.py:169
  34.9 3.7 copy-start.1
  44.6 2.9 copy-start.2
  169.8 166.6 %all-to-all-start.1 = ((bf16[16,296,768]{2,1,0:T(8,128)(2,1)}), bf16[16,296,768]{2,1,0:T(8,128)(2,1)}, u32[]{:S(2)}, u32[]{:S(2)}) async-start(bf16[16,296,768]{2,1,0:T(8,128)(2,1)} %copy-done.2), calls=%async_computation.1 | async-start | bytes 14548992 | tf_op jit(solution)/shard_map/all_to_all | solution.py:169
  218.6 140.5 %collective-permute-start.1 = (bf16[1024,768]{1,0:T(8,128)(2,1)S(1)}, bf16[1024,768]{1,0:T(8,128)(2,1)}, u32[]{:S(2)}, u32[]{:S(2)}) collective-permute-start(bf16[1024,768]{1,0:T(8,128)(2,1)S(1)} %histogram.5), channel_id=1, source_target_pairs={{0,1},{1,0},{2,3},{3,2},{4,5},{5,4},{6,7},{7,6},{8,9},{9,8},{10,11... | collective-permute-start | bytes 4718600 | tf_op jit(solution)/shard_map/ppermute | solution.py:17
  350.6 8.5 %copy-start.6 = (f32[1024]{0:T(1024)S(1)}, f32[1024]{0:T(1024)}, u32[]{:S(2)}) copy-start(f32[1024]{0:T(1024)} %param.9) | copy-start | bytes 12292
  350.6 8.5 %copy-start.7 = (f32[1024]{0:T(1024)S(1)}, f32[1024]{0:T(1024)}, u32[]{:S(2)}) copy-start(f32[1024]{0:T(1024)} %param.8) | copy-start | bytes 12292
  350.6 8.5 %collective-permute-start = (bf16[1024,768]{1,0:T(8,128)(2,1)S(1)}, bf16[1024,768]{1,0:T(8,128)(2,1)}, u32[]{:S(2)}, u32[]{:S(2)}) collective-permute-start(bf16[1024,768]{1,0:T(8,128)(2,1)S(1)} %histogram.4), channel_id=1, source_target_pairs={{0,1},{1,0},{2,3},{3,2},{4,5},{5,4},{6,7},{7,6},{8,9},{9,8},{10,11... | collective-permute-start | bytes 4718600 | tf_op jit(solution)/shard_map/ppermute | solution.py:17

commit v2 on v1

--- a/solution.py
+++ b/solution.py
@@ -9,6 +9,7 @@
 from jax.sharding import PartitionSpec as P
 
 ALIGN = 8
+MESH = pl.DeviceIdType.MESH
 
 
 def from_behind(value, axis, steps):
@@ -133,6 +134,127 @@
         ),
         name="histogram",
     )(local, rows)
+
+
+def reduce_kernel(
+    piece, shares_ref, out_ref, own, got_near, sums, got_far,
+    own_sem, near_send, near_recv, far_send, far_recv,
+):
+    far, near, rows, _ = shares_ref.shape
+    me = lax.axis_index("bins")
+    f, n = me // near, lax.rem(me, near)
+
+    def near_peer(d):
+        return lax.rem(n + d, near)
+
+    def far_peer(d):
+        return lax.rem(f + d, far)
+
+    barrier = pltpu.get_barrier_semaphore()
+    for d in range(1, near):
+        pl.semaphore_signal(
+            barrier, inc=1, device_id={"bins": f * near + near_peer(d)}, device_id_type=MESH
+        )
+    for d in range(1, far):
+        pl.semaphore_signal(
+            barrier, inc=1, device_id={"bins": far_peer(d) * near + n}, device_id_type=MESH
+        )
+    pl.semaphore_wait(barrier, near + far - 2)
+
+    def part_of(c):
+        return pl.ds(pl.multiple_of(c * piece, piece), piece)
+
+    def near_copy(d, c):
+        return pltpu.make_async_remote_copy(
+            src_ref=shares_ref.at[:, near_peer(d), part_of(c), :],
+            dst_ref=got_near.at[d - 1, :, part_of(c), :],
+            send_sem=near_send.at[d - 1, c],
+            recv_sem=near_recv.at[d - 1, c],
+            device_id={"bins": f * near + near_peer(d)},
+            device_id_type=MESH,
+        )
+
+    def far_copy(d, c):
+        return pltpu.make_async_remote_copy(
+            src_ref=sums.at[far_peer(d), part_of(c), :],
+            dst_ref=got_far.at[d - 1, part_of(c), :],
+            send_sem=far_send.at[d - 1, c],
+            recv_sem=far_recv.at[d - 1, c],
+            device_id={"bins": far_peer(d) * near + n},
+            device_id_type=MESH,
+        )
+
+    own_copy = pltpu.make_async_copy(shares_ref.at[:, n], own, own_sem)
+    own_copy.start()
+    pieces = rows // piece
+
+    @pl.loop(0, pieces)
+    def _(c):
+        for d in range(1, near):
+            near_copy(d, c).start()
+
+    own_copy.wait()
+
+    @pl.loop(0, pieces)
+    def _(c):
+        part = part_of(c)
+        for d in range(1, near):
+            near_copy(d, c).wait_recv()
+
+        @pl.loop(0, far)
+        def _(k):
+            total = own[k, part, :].astype(jnp.float32)
+            for d in range(1, near):
+                total += got_near[d - 1, k, part, :].astype(jnp.float32)
+            sums[k, part, :] = total
+
+        for d in range(1, far):
+            far_copy(d, c).start()
+
+    @pl.loop(0, pieces)
+    def _(c):
+        part = part_of(c)
+        for d in range(1, far):
+            far_copy(d, c).wait_recv()
+        total = sums[f, part, :]
+        for d in range(1, far):
+            total += got_far[d - 1, part, :]
+        out_ref[part, :] = total
+        for d in range(1, near):
+            near_copy(d, c).wait_send()
+        for d in range(1, far):
+            far_copy(d, c).wait_send()
+
+
+def reduce_shares(shares):
+    owners, rows, cols = shares.shape
+    near = math.isqrt(owners)
+    while owners % near:
+        near -= 1
+    far = owners // near
+    piece = 16 if rows % 16 == 0 else rows
+    pieces = rows // piece
+    return pl.pallas_call(
+        functools.partial(reduce_kernel, piece),
+        out_shape=jax.ShapeDtypeStruct((rows, cols), jnp.float32),
+        in_specs=[pl.BlockSpec(memory_space=pl.ANY)],
+        out_specs=pl.BlockSpec(memory_space=pltpu.VMEM),
+        scratch_shapes=[
+            pltpu.VMEM((far, rows, cols), shares.dtype),
+            pltpu.VMEM((near - 1, far, rows, cols), shares.dtype),
+            pltpu.VMEM((far, rows, cols), jnp.float32),
+            pltpu.VMEM((far - 1, rows, cols), jnp.float32),
+            pltpu.SemaphoreType.DMA,
+            pltpu.SemaphoreType.DMA((near - 1, pieces)),
+            pltpu.SemaphoreType.DMA((near - 1, pieces)),
+            pltpu.SemaphoreType.DMA((far - 1, pieces)),
+            pltpu.SemaphoreType.DMA((far - 1, pieces)),
+        ],
+        compiler_params=pltpu.CompilerParams(
+            collective_id=1, has_side_effects=True, vmem_limit_bytes=40 << 20
+        ),
+        name="reduce_shares",
+    )(shares.reshape(far, near, rows, cols))
 
 
 def body(event_bins, event_weights, nominal, background, observed):
@@ -180,8 +302,7 @@
     full = lax.dot_general(weighted, partners, dims, preferred_element_type=jnp.float32)
     full = full.astype(jnp.bfloat16)
     shares = full.reshape(owners, width_g // owners, full.shape[1])
-    got = lax.all_to_all(shares, "bins", split_axis=0, concat_axis=0, tiled=True)
-    summed = jnp.sum(got.astype(jnp.float32), axis=0)
+    summed = reduce_shares(shares)
     return summed * (1.0 / (bins_dev * owners))
 
 

time: 615 us -> 529 us (0.86)
  blocking collectives: 239 us -> 0 us
  Pallas kernels: 49.3 us -> 199 us
    all_to_all x1 -> x0, blocking collectives: 239 us -> none  [body(): lax.all_to_all(shares, 'bins', split_axis=0, concat_axis=0, tiled=True)]
    pallas_call x0 -> x1, Pallas kernels: none -> 150 us  [reduce_shares(): pl.pallas_call(functools.partial(reduce_kernel, piece), out_shape=jax.Sha...]
    unnamed x16 -> x18, local copies, waits for them, and re-layouts: 13.8 us -> 17.6 us
  transfers between devices with their start and end apart: 5 -> 5, of which waited for: 2 -> 2; matrix products, arithmetic and copies ran while one was open for 0% -> 1% of each run, Pallas kernels for 7% -> 9%
where the time goes in v2:
time: 529 us; the launch traced here: 528 us
  waiting for transfers between devices  240 us (45%)
  Pallas kernels  199 us (38%)
  starting transfers between devices  49.9 us (9%)
  local copies, waits for them, and re-layouts  20.5 us (4%)
  matrix products  13.8 us (3%)
    all_to_all x2, waiting for transfers between devices, body(): lax.all_to_all(packed, 'bins', split_axis=0, concat_axis=0, tiled=True)  240 us
    pallas_call x1, Pallas kernels, reduce_shares(): pl.pallas_call(functools.partial(reduce_kernel, piece), out_shape=jax.Sha...  150 us
    all_to_all x2, starting transfers between devices, body(): lax.all_to_all(packed, 'bins', split_axis=0, concat_axis=0, tiled=True)  41.4 us
    pallas_call x3, Pallas kernels, histogram_of(): pl.pallas_call(functools.partial(hist_kernel, math.gcd(total, 128), math....  34 us
    unnamed x18, local copies, waits for them, and re-layouts  17.6 us
    dot_general x1, matrix products, body(): lax.dot_general(weighted, partners, dims, preferred_element_type=jnp.floa...  13.8 us
    pallas_call x2, Pallas kernels, pack(): pl.pallas_call(functools.partial(pack_kernel, owners, slot, first, width)...  12 us
  transfers between devices with their start and end apart: 5, of which 2 were waited for; matrix products, arithmetic and copies ran while one was open for 1% of the time, Pallas kernels for 9%

profile of v2, /device:TPU:0, one launch (start us, length us, event | category | flops | bytes accessed | tf_op | source)
XLA Modules:
  0.0 527.7 jit_solution(3968735147014836358)
XLA Ops:
  0.0 0.7 stack.12
  0.7 0.8 fusion.17
  1.5 0.1 convert_reduce_fusion
  1.6 0.5 fusion.15.starts_ref
  2.2 0.1 pad.8.clone
  2.3 0.7 maximum_maximum_fusion.table_ref
  3.0 3.4 pack_meta.1
  6.3 8.3 %all-to-all-start = ((f32[16,2,296]{2,1,0:T(2,128)}), f32[16,2,296]{2,1,0:T(2,128)S(1)}, u32[]{:S(2)}, u32[]{:S(2)}) async-start(f32[16,2,296]{2,1,0:T(2,128)} %pack_meta.1), calls=%async_computation | async-start | bytes 98304 | tf_op jit(solution)/shard_map/all_to_all | solution.py:280
  14.7 0.0 copy-start
  14.7 3.7 copy-done
  18.4 0.0 copy-start.5
  18.4 0.6 copy-done.5
  19.0 6.0 %pack.3 = bf16[16,296,768]{2,1,0:T(8,128)(2,1)S(1)} custom-call(s32[16]{0:T(128)S(1)} %copy-done.5, bf16[3072,1536]{1,0:T(8,128)(2,1)S(1)} %copy-done), custom_call_target="tpu_custom_call" | custom-call | bytes 14548992 | tf_op jit(solution)/shard_map/pack/pallas_call | solution.py:47
  25.0 0.0 copy-start.3
  25.0 3.0 copy-done.3
  28.0 0.0 copy-start.6
  28.0 0.0 all-to-all-done
  28.0 7.0 %all-to-all-start.2 = ((bf16[16,296,768]{2,1,0:T(8,128)(2,1)}), bf16[16,296,768]{2,1,0:T(8,128)(2,1)}, u32[]{:S(2)}, u32[]{:S(2)}) async-start(bf16[16,296,768]{2,1,0:T(8,128)(2,1)} %copy-done.3), calls=%async_computation.2 | async-start | bytes 14548992 | tf_op jit(solution)/shard_map/all_to_all | solution.py:291
  35.0 0.0 copy-done.6
  35.0 0.0 copy-start.1
  35.0 3.7 copy-done.1
  38.7 6.0 %pack.2 = bf16[16,296,768]{2,1,0:T(8,128)(2,1)S(1)} custom-call(s32[16]{0:T(128)S(1)} %copy-done.6, bf16[3072,1536]{1,0:T(8,128)(2,1)S(1)} %copy-done.1), custom_call_target="tpu_custom_call" | custom-call | bytes 14548992 | tf_op jit(solution)/shard_map/pack/pallas_call | solution.py:47
  44.6 0.0 copy-start.2
  44.7 2.9 copy-done.2
  47.6 122.3 %all-to-all-done.2 = bf16[16,296,768]{2,1,0:T(8,128)(2,1)} async-done(((bf16[16,296,768]{2,1,0:T(8,128)(2,1)}), bf16[16,296,768]{2,1,0:T(8,128)(2,1)}, u32[]{:S(2)}, u32[]{:S(2)}) %all-to-all-start.2) | async-done | bytes 7274528 | tf_op jit(solution)/shard_map/all_to_all | solution.py:291
  169.9 34.4 %all-to-all-start.1 = ((bf16[16,296,768]{2,1,0:T(8,128)(2,1)}), bf16[16,296,768]{2,1,0:T(8,128)(2,1)}, u32[]{:S(2)}, u32[]{:S(2)}) async-start(bf16[16,296,768]{2,1,0:T(8,128)(2,1)} %copy-done.2), calls=%async_computation.1 | async-start | bytes 14548992 | tf_op jit(solution)/shard_map/all_to_all | solution.py:291
  204.3 0.1 fusion.12
  204.4 0.1 convert_element_type.40.local_ref
  204.5 14.1 %histogram.5 = bf16[1024,768]{1,0:T(8,128)(2,1)S(1)} custom-call(s32[1,4736]{1,0:T(1,128)S(1)} %convert_element_type.40.local_ref, bf16[4736,768]{1,0:T(8,128)(2,1)} %bitcast.3.rows_ref), custom_call_target="tpu_custom_call" | custom-call | flops 7449083904 | bytes 7274496 | tf_op jit(solution)/shard_map/histogram/pallas_call | solution.py:119
  218.7 0.1 collective-permute-start.1
  218.7 117.7 %all-to-all-done.1 = bf16[16,296,768]{2,1,0:T(8,128)(2,1)} async-done(((bf16[16,296,768]{2,1,0:T(8,128)(2,1)}), bf16[16,296,768]{2,1,0:T(8,128)(2,1)}, u32[]{:S(2)}, u32[]{:S(2)}) %all-to-all-start.1) | async-done | bytes 7274528 | tf_op jit(solution)/shard_map/all_to_all | solution.py:291
  336.5 14.2 %histogram.4 = bf16[1024,768]{1,0:T(8,128)(2,1)S(1)} custom-call(s32[1,4736]{1,0:T(1,128)S(1)} %convert_element_type.40.local_ref, bf16[4736,768]{1,0:T(8,128)(2,1)} %bitcast.2.rows_ref), custom_call_target="tpu_custom_call" | custom-call | flops 7449083904 | bytes 7274496 | tf_op jit(solution)/shard_map/histogram/pallas_call | solution.py:119
  350.7 0.0 copy-start.7
  350.7 0.0 copy-start.8
  350.7 0.1 collective-permute-start
  350.8 0.1 fusion.11
  350.8 0.1 convert_element_type.41
  351.0 2.3 broadcast_in_dim.5.rows_ref
  353.3 5.6 %histogram.3 = f32[1024,128]{1,0:T(8,128)S(1)} custom-call(s32[1,4736]{1,0:T(1,128)S(1)} %convert_element_type.40.local_ref, bf16[4736,128]{1,0:T(8,128)(2,1)S(1)} %broadcast_in_dim.5.rows_ref), custom_call_target="tpu_custom_call" | custom-call | flops 1241513984 | bytes 1212416 | tf_op jit(solution)/shard_map/histogram/pallas_call | solution.py:119
  358.9 0.2 slice_reduce_fusion
  359.2 0.0 copy-done.7
  359.2 0.0 copy-done.8
  359.2 0.0 collective-permute-done.1
  359.2 0.0 collective-permute-done
  359.2 13.8 %convolution_convert_fusion = bf16[1536,3072]{1,0:T(8,128)(2,1)} fusion(bf16[1024,768]{1,0:T(8,128)(2,1)} %collective-permute-done.1, bf16[1024,768]{1,0:T(8,128)(2,1)} %collective-permute-done, bf16[1024,768]{1,0:T(8,128)(2,1)S(1)} %histogram.5, bf16[1024,768]{1,0:T(8,128)(2,1)S(1)} %histogram.4, f32[1024]{0:T(1024)S(1)} %multiply_divide_fusion), kind=kOutput, calls=%fused_computation | convolution fusion | flops 9702998016 | bytes 15732736 | tf_op jit(solution)/shard_map/dot_general | solution.py:302
  373.0 0.0 copy-start.4
  373.1 3.7 copy-done.4
  376.7 149.8 %reduce_shares.1 = f32[96,3072]{1,0:T(8,128)S(1)} custom-call(bf16[4,4,96,3072]{3,2,1,0:T(8,128)(2,1)S(1)} %bitcast.5), custom_call_target="tpu_custom_call" | custom-call | tf_op jit(solution)/shard_map/reduce_shares/pallas_call | solution.py:237
  526.6 1.1 broadcast_multiply_fusion
  (2 shorter events, 0.0 us)
Async XLA Ops:
  6.3 21.7 %all-to-all-start = ((f32[16,2,296]{2,1,0:T(2,128)}), f32[16,2,296]{2,1,0:T(2,128)S(1)}, u32[]{:S(2)}, u32[]{:S(2)}) async-start(f32[16,2,296]{2,1,0:T(2,128)} %pack_meta.1), calls=%async_computation | async-start | bytes 98304 | tf_op jit(solution)/shard_map/all_to_all | solution.py:280
  14.7 3.7 copy-start
  18.4 0.6 copy-start.5
  25.0 3.0 copy-start.3
  28.0 7.0 %copy-start.6 = (s32[16]{0:T(128)S(1)}, s32[16]{0:T(128)}, u32[]{:S(2)}) copy-start(s32[16]{0:T(128)} %fusion.15.starts_ref) | copy-start | bytes 196
  28.0 141.9 %all-to-all-start.2 = ((bf16[16,296,768]{2,1,0:T(8,128)(2,1)}), bf16[16,296,768]{2,1,0:T(8,128)(2,1)}, u32[]{:S(2)}, u32[]{:S(2)}) async-start(bf16[16,296,768]{2,1,0:T(8,128)(2,1)} %copy-done.3), calls=%async_computation.2 | async-start | bytes 14548992 | tf_op jit(solution)/shard_map/all_to_all | solution.py:291
  35.0 3.7 copy-start.1
  44.6 2.9 copy-start.2
  169.9 166.6 %all-to-all-start.1 = ((bf16[16,296,768]{2,1,0:T(8,128)(2,1)}), bf16[16,296,768]{2,1,0:T(8,128)(2,1)}, u32[]{:S(2)}, u32[]{:S(2)}) async-start(bf16[16,296,768]{2,1,0:T(8,128)(2,1)} %copy-done.2), calls=%async_computation.1 | async-start | bytes 14548992 | tf_op jit(solution)/shard_map/all_to_all | solution.py:291
  218.7 140.5 %collective-permute-start.1 = (bf16[1024,768]{1,0:T(8,128)(2,1)S(1)}, bf16[1024,768]{1,0:T(8,128)(2,1)}, u32[]{:S(2)}, u32[]{:S(2)}) collective-permute-start(bf16[1024,768]{1,0:T(8,128)(2,1)S(1)} %histogram.5), channel_id=1, source_target_pairs={{0,1},{1,0},{2,3},{3,2},{4,5},{5,4},{6,7},{7,6},{8,9},{9,8},{10,11... | collective-permute-start | bytes 4718600 | tf_op jit(solution)/shard_map/ppermute | solution.py:18
  350.7 8.5 %copy-start.7 = (f32[1024]{0:T(1024)S(1)}, f32[1024]{0:T(1024)}, u32[]{:S(2)}) copy-start(f32[1024]{0:T(1024)} %param.9) | copy-start | bytes 12292
  350.7 8.5 %copy-start.8 = (f32[1024]{0:T(1024)S(1)}, f32[1024]{0:T(1024)}, u32[]{:S(2)}) copy-start(f32[1024]{0:T(1024)} %param.8) | copy-start | bytes 12292
  350.7 8.5 %collective-permute-start = (bf16[1024,768]{1,0:T(8,128)(2,1)S(1)}, bf16[1024,768]{1,0:T(8,128)(2,1)}, u32[]{:S(2)}, u32[]{:S(2)}) collective-permute-start(bf16[1024,768]{1,0:T(8,128)(2,1)S(1)} %histogram.4), channel_id=1, source_target_pairs={{0,1},{1,0},{2,3},{3,2},{4,5},{5,4},{6,7},{7,6},{8,9},{9,8},{10,11... | collective-permute-start | bytes 4718600 | tf_op jit(solution)/shard_map/ppermute | solution.py:18
  373.0 3.7 copy-start.4

commit v3 on v2

--- a/solution.py
+++ b/solution.py
@@ -57,7 +57,7 @@
             pltpu.SemaphoreType.DMA((owners,)),
             pltpu.SemaphoreType.DMA((owners,)),
         ],
-        compiler_params=pltpu.CompilerParams(vmem_limit_bytes=32 << 20),
+        compiler_params=pltpu.CompilerParams(vmem_limit_bytes=56 << 20),
         cost_estimate=pl.CostEstimate(
             flops=0, bytes_accessed=4 * owners * slot * width, transcendentals=0
         ),
@@ -94,46 +94,103 @@
     )(starts, table)
 
 
-def hist_kernel(chunk, tile, local_ref, rows_ref, out_ref, hot):
-    bins, total = hot.shape
-
-    @pl.when(pl.program_id(0) == 0)
-    def _():
-        ids = lax.broadcasted_iota(jnp.int32, (bins, chunk), 0)
-
-        @pl.loop(0, total // chunk)
-        def _(k):
-            part = pl.ds(pl.multiple_of(k * chunk, chunk), chunk)
-            hot[:, part] = (ids == local_ref[:, part]).astype(jnp.bfloat16)
+def gather_kernel(
+    tile, block, meta_ref, packed_ref, out_ref, nominal_ref, total, own, held,
+    own_sem, send_sems, recv_sems,
+):
+    owners, slot, width = packed_ref.shape
+    bins = total.shape[0]
+    me = lax.axis_index("bins")
+
+    barrier = pltpu.get_barrier_semaphore()
+
+    @pl.loop(1, owners)
+    def _(d):
+        pl.semaphore_signal(
+            barrier, inc=1, device_id={"bins": lax.rem(me + d, owners)}, device_id_type=MESH
+        )
+
+    pl.semaphore_wait(barrier, owners - 1)
+
+    def offset(i):
+        return owners // 2 + ((i + 1) // 2) * (1 - 2 * lax.rem(i, 2))
+
+    def copy_of(i):
+        target = lax.rem(me + offset(i), owners)
+        return pltpu.make_async_remote_copy(
+            src_ref=packed_ref.at[target],
+            dst_ref=held.at[i],
+            send_sem=send_sems.at[i],
+            recv_sem=recv_sems.at[i],
+            device_id={"bins": target},
+            device_id_type=MESH,
+        )
+
+    @pl.loop(0, owners - 1)
+    def _(i):
+        copy_of(i).start()
+
+    own_copy = pltpu.make_async_copy(packed_ref.at[me], own, own_sem)
+    own_copy.start()
+    own_copy.wait()
+
+    def add(source, rows, first):
+        @pl.loop(0, bins // tile)
+        def _(m):
+            base = pl.multiple_of(m * tile, tile)
+            part = pl.ds(base, tile)
+            ids = (lax.broadcasted_iota(jnp.int32, (tile, slot), 0) + base).astype(jnp.float32)
+            same = ids == meta_ref[source, 0:1, :]
+            hot = same.astype(jnp.bfloat16)
+            picked = jnp.where(same, meta_ref[source, 1:2, :], 0.0)
+            sums = jnp.sum(picked, axis=1, keepdims=True)
+            nominal_ref[part, :] = sums if first else nominal_ref[part, :] + sums
+            for j in range(width // block):
+                cols = pl.ds(j * block, block)
+                value = jnp.dot(hot, rows[:, cols], preferred_element_type=jnp.float32)
+                total[part, cols] = value if first else total[part, cols] + value
+
+    add(me, own, True)
+
+    @pl.loop(0, owners - 1)
+    def _(i):
+        copy_of(i).wait_recv()
+        add(lax.rem(me - offset(i) + owners, owners), held.at[i], False)
 
     @pl.loop(0, bins // tile)
     def _(m):
         part = pl.ds(pl.multiple_of(m * tile, tile), tile)
-        out_ref[part, :] = jnp.dot(
-            hot[part, :], rows_ref[...], preferred_element_type=jnp.float32
-        ).astype(out_ref.dtype)
-
-
-def histogram_of(local, rows, bins, block, dtype):
-    total, width = rows.shape
+        out_ref[part, :] = total[part, :].astype(out_ref.dtype)
+
+    @pl.loop(0, owners - 1)
+    def _(i):
+        copy_of(i).wait_send()
+
+
+def gather_histogram(meta, packed, bins):
+    owners, slot, width = packed.shape
+    vmem = pl.BlockSpec(memory_space=pltpu.VMEM)
     return pl.pallas_call(
-        functools.partial(hist_kernel, math.gcd(total, 128), math.gcd(bins, 256)),
-        grid=(width // block,),
-        out_shape=jax.ShapeDtypeStruct((bins, width), dtype),
-        in_specs=[
-            pl.BlockSpec((1, total), lambda j: (0, 0)),
-            pl.BlockSpec((total, block), lambda j: (0, j)),
-        ],
-        out_specs=pl.BlockSpec((bins, block), lambda j: (0, j)),
-        scratch_shapes=[pltpu.VMEM((bins, total), jnp.bfloat16)],
+        functools.partial(gather_kernel, math.gcd(bins, 256), math.gcd(width, 512)),
+        out_shape=(
+            jax.ShapeDtypeStruct((bins, width), jnp.bfloat16),
+            jax.ShapeDtypeStruct((bins, 1), jnp.float32),
+        ),
+        in_specs=[vmem, pl.BlockSpec(memory_space=pl.ANY)],
+        out_specs=(vmem, vmem),
+        scratch_shapes=[
+            pltpu.VMEM((bins, width), jnp.float32),
+            pltpu.VMEM((slot, width), packed.dtype),
+            pltpu.VMEM((owners - 1, slot, width), packed.dtype),
+            pltpu.SemaphoreType.DMA,
+            pltpu.SemaphoreType.DMA((owners - 1,)),
+            pltpu.SemaphoreType.DMA((owners - 1,)),
+        ],
         compiler_params=pltpu.CompilerParams(
-            vmem_limit_bytes=40 << 20, dimension_semantics=("arbitrary",)
+            collective_id=2, has_side_effects=True, vmem_limit_bytes=56 << 20
         ),
-        cost_estimate=pl.CostEstimate(
-            flops=2 * bins * total * width, bytes_accessed=2 * total * width, transcendentals=0
-        ),
-        name="histogram",
-    )(local, rows)
+        name="gather_histogram",
+    )(meta, packed)
 
 
 def reduce_kernel(
@@ -251,7 +308,7 @@
             pltpu.SemaphoreType.DMA((far - 1, pieces)),
         ],
         compiler_params=pltpu.CompilerParams(
-            collective_id=1, has_side_effects=True, vmem_limit_bytes=40 << 20
+            collective_id=1, has_side_effects=True, vmem_limit_bytes=56 << 20
         ),
         name="reduce_shares",
     )(shares.reshape(far, near, rows, cols))
@@ -265,10 +322,6 @@
     bins_dev = background.shape[0]
     capacity = 3 * events // (2 * owners)
     slot = -(-capacity // ALIGN) * ALIGN + ALIGN
-    chunks = 2 if width_g % 512 == 0 else 1
-    width = width_g // chunks
-    block = math.gcd(width, 256)
-
     destination = event_bins // bins_dev
     targets = jnp.arange(owners, dtype=jnp.int32)
     before = jnp.sum((destination[None, :] < targets[:, None]).astype(jnp.int32), axis=1)
@@ -278,25 +331,14 @@
     table = jnp.concatenate([table, jnp.zeros((6, events), jnp.float32)], axis=0)
     meta = pack_meta(starts, table, slot, bins_dev)
     got_meta = lax.all_to_all(meta, "bins", split_axis=0, concat_axis=0, tiled=True)
-    local = got_meta[:, 0].astype(jnp.int32).reshape(1, owners * slot)
-    got_nominal = got_meta[:, 1].astype(jnp.bfloat16).reshape(owners * slot, 1)
-    got_nominal = jnp.broadcast_to(got_nominal, (owners * slot, 128))
-    nominal_sum = histogram_of(local, got_nominal, bins_dev, 128, jnp.float32)[:, 0]
-    yields = background + nominal_sum
+    packed = pack(starts, event_weights, slot, 0, width_g)
+    templates, nominal_sum = gather_histogram(got_meta, packed, bins_dev)
+    yields = background + nominal_sum[:, 0]
     curvature = observed / (yields * yields)
-
-    parts = []
-    for c in range(chunks):
-        packed = pack(starts, event_weights, slot, c * width, width)
-        got = lax.all_to_all(packed, "bins", split_axis=0, concat_axis=0, tiled=True)
-        got = got.reshape(owners * slot, width)
-        parts.append(histogram_of(local, got, bins_dev, block, jnp.bfloat16))
-    templates = jnp.concatenate(parts, axis=1)
     weighted = (curvature[:, None] * templates.astype(jnp.float32)).astype(jnp.bfloat16)
     pieces = [templates]
     for shift_by in range(1, groups_count // 2 + 1):
-        shifted = [from_behind(part, "params", -shift_by) for part in parts]
-        pieces.append(jnp.concatenate(shifted, axis=1))
+        pieces.append(from_behind(templates, "params", -shift_by))
     partners = jnp.concatenate(pieces, axis=1)
     dims = (((0,), (0,)), ((), ()))
     full = lax.dot_general(weighted, partners, dims, preferred_element_type=jnp.float32)

time: 529 us -> 554 us (1.047); the launches traced: 528 us -> 546 us
  Pallas kernels: 199 us -> 511 us
  waiting for transfers between devices: 240 us -> 4.58 us
  starting transfers between devices: 49.9 us -> 8.41 us
  local copies, waits for them, and re-layouts: 20.5 us -> 0.71 us
    pallas_call x3 -> x1, Pallas kernels: 34 us -> 314 us  [gather_histogram(): pl.pallas_call(functools.partial(gather_kernel, math.gcd(bins, 256), math...]
    all_to_all x2 -> x0, waiting for transfers between devices: 240 us -> none  [body(): lax.all_to_all(packed, 'bins', split_axis=0, concat_axis=0, tiled=True)]
    all_to_all x2 -> x0, starting transfers between devices: 41.4 us -> none  [body(): lax.all_to_all(packed, 'bins', split_axis=0, concat_axis=0, tiled=True)]
    pallas_call x1, Pallas kernels: 150 us -> 181 us  [reduce_shares(): pl.pallas_call(functools.partial(reduce_kernel, piece), out_shape=jax.Sha...]
    unnamed x18 -> x6, local copies, waits for them, and re-layouts: 17.6 us -> 0.63 us
    pallas_call x2 -> x1, Pallas kernels: 12 us -> 11.5 us  [pack(): pl.pallas_call(functools.partial(pack_kernel, owners, slot, first, width)...]
  transfers between devices with their start and end apart: 5 -> 2, of which waited for: 2 -> 1; matrix products, arithmetic and copies ran while one was open for 1% -> 0% of each run, Pallas kernels for 9% -> 2%
where the time goes in v3:
time: 554 us; the launch traced here: 546 us
  Pallas kernels  511 us (92%)
  matrix products  15 us (3%)
  starting transfers between devices  8.41 us (2%)
  other arithmetic  6.49 us (1%)
    pallas_call x1, Pallas kernels, gather_histogram(): pl.pallas_call(functools.partial(gather_kernel, math.gcd(bins, 256), math...  314 us
    pallas_call x1, Pallas kernels, reduce_shares(): pl.pallas_call(functools.partial(reduce_kernel, piece), out_shape=jax.Sha...  181 us
    dot_general x1, matrix products, body(): lax.dot_general(weighted, partners, dims, preferred_element_type=jnp.floa...  15 us
    pallas_call x1, Pallas kernels, pack(): pl.pallas_call(functools.partial(pack_kernel, owners, slot, first, width)...  11.5 us
  transfers between devices with their start and end apart: 2, of which 1 were waited for; matrix products, arithmetic and copies ran while one was open for 0% of the time, Pallas kernels for 2%

profile of v3, /device:TPU:0, one launch (start us, length us, event | category | flops | bytes accessed | tf_op | source)
XLA Modules:
  0.0 546.1 jit_solution(2370155494514318022)
XLA Ops:
  0.0 0.7 stack.12
  0.7 0.8 fusion.8
  1.5 0.1 convert_reduce_fusion
  1.6 0.5 fusion.6.starts_ref
  2.1 0.1 pad.4.clone
  2.2 0.7 maximum_maximum_fusion.table_ref
  2.9 3.4 pack_meta.1
  6.3 8.3 %all-to-all-start = ((f32[16,2,296]{2,1,0:T(2,128)}), f32[16,2,296]{2,1,0:T(2,128)S(1)}, u32[]{:S(2)}, u32[]{:S(2)}) async-start(f32[16,2,296]{2,1,0:T(2,128)} %pack_meta.1), calls=%async_computation | async-start | bytes 98304 | tf_op jit(solution)/shard_map/all_to_all | solution.py:333
  14.7 11.5 %pack.1.packed_ref = bf16[16,296,1536]{2,1,0:T(8,128)(2,1)} custom-call(s32[16]{0:T(128)} %fusion.6.starts_ref, bf16[3072,1536]{1,0:T(8,128)(2,1)} %rows_ref.1), custom_call_target="tpu_custom_call" | custom-call | bytes 29097984 | tf_op jit(solution)/shard_map/pack/pallas_call | solution.py:47
  26.2 0.0 copy-start.1
  26.2 0.0 copy-start.2
  26.2 0.0 all-to-all-done.meta_ref
  26.2 0.0 copy-start
  26.2 0.6 copy-done
  26.9 314.4 %gather_histogram.1 = (bf16[1024,1536]{1,0:T(8,128)(2,1)}, f32[1024,1]{1,0:T(8,128)}) custom-call(f32[16,2,296]{2,1,0:T(2,128)} %copy-done, bf16[16,296,1536]{2,1,0:T(8,128)(2,1)} %pack.1.packed_ref), custom_call_target="tpu_custom_call" | custom-call | tf_op jit(solution)/shard_map/gather_histogram/pallas_call | solution.py:173
  341.3 0.1 collective-permute-start
  341.4 1.2 reduce
  342.6 0.0 copy-done.1
  342.6 0.0 copy-done.2
  342.7 4.6 collective-permute-done
  347.2 15.0 %convolution_convert_fusion = bf16[1536,3072]{1,0:T(8,128)(2,1)} fusion(bf16[1024,1536]{1,0:T(8,128)(2,1)S(1)} %collective-permute-done, bf16[1024,1536]{1,0:T(8,128)(2,1)} %get-tuple-element.8, f32[1024]{0:T(1024)S(1)} %multiply_divide_fusion), kind=kOutput, calls=%fused_computation | convolution fusion | flops 9685696512 | bytes 15732736 | tf_op jit(solution)/shard_map/dot_general | solution.py:344
  362.2 181.5 %reduce_shares.1 = f32[96,3072]{1,0:T(8,128)} custom-call(bf16[4,4,96,3072]{3,2,1,0:T(8,128)(2,1)} %bitcast.3), custom_call_target="tpu_custom_call" | custom-call | tf_op jit(solution)/shard_map/reduce_shares/pallas_call | solution.py:294
  543.7 2.4 broadcast_multiply_fusion
  (2 shorter events, 0.0 us)
Async XLA Ops:
  6.3 19.9 %all-to-all-start = ((f32[16,2,296]{2,1,0:T(2,128)}), f32[16,2,296]{2,1,0:T(2,128)S(1)}, u32[]{:S(2)}, u32[]{:S(2)}) async-start(f32[16,2,296]{2,1,0:T(2,128)} %pack_meta.1), calls=%async_computation | async-start | bytes 98304 | tf_op jit(solution)/shard_map/all_to_all | solution.py:333
  26.2 316.4 %copy-start.1 = (f32[1024]{0:T(1024)S(1)}, f32[1024]{0:T(1024)}, u32[]{:S(2)}) copy-start(f32[1024]{0:T(1024)} %param.9) | copy-start | bytes 12292
  26.2 316.4 %copy-start.2 = (f32[1024]{0:T(1024)S(1)}, f32[1024]{0:T(1024)}, u32[]{:S(2)}) copy-start(f32[1024]{0:T(1024)} %param.8) | copy-start | bytes 12292
  26.2 0.6 copy-start
  341.3 5.9 %collective-permute-start = (bf16[1024,1536]{1,0:T(8,128)(2,1)}, bf16[1024,1536]{1,0:T(8,128)(2,1)S(1)}, u32[]{:S(2)}, u32[]{:S(2)}) collective-permute-start(bf16[1024,1536]{1,0:T(8,128)(2,1)} %get-tuple-element.8), channel_id=1, source_target_pairs={{0,1},{1,0},{2,3},{3,2},{4,5},{5,4},{6,7},{7,6},{8,9},{9,8},{10,11... | collective-permute-start | bytes 9437192 | tf_op jit(solution)/shard_map/ppermute | solution.py:18

commit v4 on v2

--- a/solution.py
+++ b/solution.py
@@ -57,7 +57,7 @@
             pltpu.SemaphoreType.DMA((owners,)),
             pltpu.SemaphoreType.DMA((owners,)),
         ],
-        compiler_params=pltpu.CompilerParams(vmem_limit_bytes=32 << 20),
+        compiler_params=pltpu.CompilerParams(vmem_limit_bytes=56 << 20),
         cost_estimate=pl.CostEstimate(
             flops=0, bytes_accessed=4 * owners * slot * width, transcendentals=0
         ),
@@ -127,7 +127,7 @@
         out_specs=pl.BlockSpec((bins, block), lambda j: (0, j)),
         scratch_shapes=[pltpu.VMEM((bins, total), jnp.bfloat16)],
         compiler_params=pltpu.CompilerParams(
-            vmem_limit_bytes=40 << 20, dimension_semantics=("arbitrary",)
+            vmem_limit_bytes=56 << 20, dimension_semantics=("arbitrary",)
         ),
         cost_estimate=pl.CostEstimate(
             flops=2 * bins * total * width, bytes_accessed=2 * total * width, transcendentals=0
@@ -251,7 +251,7 @@
             pltpu.SemaphoreType.DMA((far - 1, pieces)),
         ],
         compiler_params=pltpu.CompilerParams(
-            collective_id=1, has_side_effects=True, vmem_limit_bytes=40 << 20
+            collective_id=1, has_side_effects=True, vmem_limit_bytes=56 << 20
         ),
         name="reduce_shares",
     )(shares.reshape(far, near, rows, cols))
@@ -265,7 +265,7 @@
     bins_dev = background.shape[0]
     capacity = 3 * events // (2 * owners)
     slot = -(-capacity // ALIGN) * ALIGN + ALIGN
-    chunks = 2 if width_g % 512 == 0 else 1
+    chunks = 1
     width = width_g // chunks
     block = math.gcd(width, 256)
 
@@ -282,15 +282,15 @@
     got_nominal = got_meta[:, 1].astype(jnp.bfloat16).reshape(owners * slot, 1)
     got_nominal = jnp.broadcast_to(got_nominal, (owners * slot, 128))
     nominal_sum = histogram_of(local, got_nominal, bins_dev, 128, jnp.float32)[:, 0]
-    yields = background + nominal_sum
-    curvature = observed / (yields * yields)
-
     parts = []
     for c in range(chunks):
         packed = pack(starts, event_weights, slot, c * width, width)
         got = lax.all_to_all(packed, "bins", split_axis=0, concat_axis=0, tiled=True)
+        got, nominal_sum = lax.optimization_barrier((got, nominal_sum))
         got = got.reshape(owners * slot, width)
         parts.append(histogram_of(local, got, bins_dev, block, jnp.bfloat16))
+    yields = background + nominal_sum
+    curvature = observed / (yields * yields)
     templates = jnp.concatenate(parts, axis=1)
     weighted = (curvature[:, None] * templates.astype(jnp.float32)).astype(jnp.bfloat16)
     pieces = [templates]

time: 529 us -> 537 us (1.015)
  starting transfers between devices: 49.9 us -> 15.3 us
  Pallas kernels: 199 us -> 226 us
  waiting for transfers between devices: 240 us -> 265 us
  local copies, waits for them, and re-layouts: 20.5 us -> 5.47 us
    all_to_all x2 -> x1, starting transfers between devices: 41.4 us -> 6.96 us  [body(): lax.all_to_all(packed, 'bins', split_axis=0, concat_axis=0, tiled=True)]
    pallas_call x1, Pallas kernels: 150 us -> 179 us  [reduce_shares(): pl.pallas_call(functools.partial(reduce_kernel, piece), out_shape=jax.Sha...]
    all_to_all x2 -> x1, waiting for transfers between devices: 240 us -> 260 us  [body(): lax.all_to_all(packed, 'bins', split_axis=0, concat_axis=0, tiled=True)]
    unnamed x18 -> x4, local copies, waits for them, and re-layouts: 17.6 us -> 0.01 us
    ppermute x2 -> x1, waiting for transfers between devices: 0.01 us -> 5.85 us  [from_behind(): return lax.ppermute(value, axis, pairs)]
    pallas_call x3 -> x2, Pallas kernels: 34 us -> 32.5 us  [histogram_of(): pl.pallas_call(functools.partial(hist_kernel, math.gcd(total, 128), math....]
    pallas_call x2 -> x1, Pallas kernels: 12 us -> 11.5 us  [pack(): pl.pallas_call(functools.partial(pack_kernel, owners, slot, first, width)...]
  transfers between devices with their start and end apart: 5 -> 3, of which waited for: 2 -> 2; matrix products, arithmetic and copies ran while one was open for 1% -> 1% of each run, Pallas kernels for 9% -> 4%
where the time goes in v4:
time: 537 us; the launch traced here: 533 us
  waiting for transfers between devices  265 us (49%)
  Pallas kernels  226 us (42%)
  starting transfers between devices  15.3 us (3%)
  matrix products  15.2 us (3%)
  local copies, waits for them, and re-layouts  5.47 us (1%)
    all_to_all x1, waiting for transfers between devices, body(): lax.all_to_all(packed, 'bins', split_axis=0, concat_axis=0, tiled=True)  260 us
    pallas_call x1, Pallas kernels, reduce_shares(): pl.pallas_call(functools.partial(reduce_kernel, piece), out_shape=jax.Sha...  179 us
    pallas_call x2, Pallas kernels, histogram_of(): pl.pallas_call(functools.partial(hist_kernel, math.gcd(total, 128), math....  32.5 us
    dot_general x1, matrix products, body(): lax.dot_general(weighted, partners, dims, preferred_element_type=jnp.floa...  15.2 us
    pallas_call x1, Pallas kernels, pack(): pl.pallas_call(functools.partial(pack_kernel, owners, slot, first, width)...  11.5 us
  transfers between devices with their start and end apart: 3, of which 2 were waited for; matrix products, arithmetic and copies ran while one was open for 1% of the time, Pallas kernels for 4%

profile of v4, /device:TPU:0, one launch (start us, length us, event | category | flops | bytes accessed | tf_op | source)
XLA Modules:
  0.0 532.7 jit_solution(2498045427321597322)
XLA Ops:
  0.0 0.7 stack.12
  0.7 0.8 fusion.10
  1.5 0.1 convert_reduce_fusion
  1.6 0.5 fusion.8.starts_ref
  2.2 0.1 pad.4.clone
  2.2 0.7 maximum_maximum_fusion.table_ref
  3.0 3.4 pack_meta.1
  6.3 8.3 %all-to-all-start.1 = ((f32[16,2,296]{2,1,0:T(2,128)}), f32[16,2,296]{2,1,0:T(2,128)S(1)}, u32[]{:S(2)}, u32[]{:S(2)}) async-start(f32[16,2,296]{2,1,0:T(2,128)} %pack_meta.1), calls=%async_computation.1 | async-start | bytes 98304 | tf_op jit(solution)/shard_map/all_to_all | solution.py:280
  14.7 11.5 %pack.1 = bf16[16,296,1536]{2,1,0:T(8,128)(2,1)} custom-call(s32[16]{0:T(128)} %fusion.8.starts_ref, bf16[3072,1536]{1,0:T(8,128)(2,1)} %rows_ref.1), custom_call_target="tpu_custom_call" | custom-call | bytes 29097984 | tf_op jit(solution)/shard_map/pack/pallas_call | solution.py:47
  26.2 0.0 all-to-all-done.1
  26.2 7.0 %all-to-all-start = ((bf16[16,296,1536]{2,1,0:T(8,128)(2,1)}), bf16[16,296,1536]{2,1,0:T(8,128)(2,1)}, u32[]{:S(2)}, u32[]{:S(2)}) async-start(bf16[16,296,1536]{2,1,0:T(8,128)(2,1)} %pack.1), calls=%async_computation | async-start | bytes 29097984 | tf_op jit(solution)/shard_map/all_to_all | solution.py:288
  33.2 0.1 fusion.5
  33.3 0.7 convert_element_type.40.local_ref
  34.0 0.1 fusion.4
  34.1 0.1 convert_element_type.41
  34.2 3.2 broadcast_in_dim.5.rows_ref
  37.4 7.7 %histogram.2 = f32[1024,128]{1,0:T(8,128)} custom-call(s32[1,4736]{1,0:T(1,128)} %convert_element_type.40.local_ref, bf16[4736,128]{1,0:T(8,128)(2,1)} %broadcast_in_dim.5.rows_ref), custom_call_target="tpu_custom_call" | custom-call | flops 1241513984 | bytes 1212416 | tf_op jit(solution)/shard_map/histogram/pallas_call | solution.py:119
  45.2 1.2 slice_reduce_fusion
  46.4 259.5 %all-to-all-done = bf16[16,296,1536]{2,1,0:T(8,128)(2,1)} async-done(((bf16[16,296,1536]{2,1,0:T(8,128)(2,1)}), bf16[16,296,1536]{2,1,0:T(8,128)(2,1)}, u32[]{:S(2)}, u32[]{:S(2)}) %all-to-all-start) | async-done | bytes 14549024 | tf_op jit(solution)/shard_map/all_to_all | solution.py:288
  305.9 0.0 copy-start
  305.9 0.0 copy-start.1
  305.9 24.8 %histogram.3 = bf16[1024,1536]{1,0:T(8,128)(2,1)} custom-call(s32[1,4736]{1,0:T(1,128)} %convert_element_type.40.local_ref, bf16[4736,1536]{1,0:T(8,128)(2,1)} %bitcast.2.rows_ref), custom_call_target="tpu_custom_call" | custom-call | flops 14898167808 | bytes 14548992 | tf_op jit(solution)/shard_map/histogram/pallas_call | solution.py:119
  330.7 0.0 collective-permute-start
  330.7 0.0 copy-done
  330.7 0.0 copy-done.1
  330.7 5.8 %collective-permute-done = bf16[1024,1536]{1,0:T(8,128)(2,1)S(1)} collective-permute-done((bf16[1024,1536]{1,0:T(8,128)(2,1)}, bf16[1024,1536]{1,0:T(8,128)(2,1)S(1)}, u32[]{:S(2)}, u32[]{:S(2)}) %collective-permute-start) | collective-permute-done | bytes 3145760 | tf_op jit(solution)/shard_map/ppermute | solution.py:18
  336.6 15.2 %convolution_convert_fusion = bf16[1536,3072]{1,0:T(8,128)(2,1)} fusion(bf16[1024,1536]{1,0:T(8,128)(2,1)S(1)} %collective-permute-done, bf16[1024,1536]{1,0:T(8,128)(2,1)} %histogram.3, f32[1024]{0:T(1024)S(1)} %multiply_divide_fusion), kind=kOutput, calls=%fused_computation | convolution fusion | flops 9685696512 | bytes 15732736 | tf_op jit(solution)/shard_map/dot_general | solution.py:302
  351.8 178.6 %reduce_shares.1 = f32[96,3072]{1,0:T(8,128)} custom-call(bf16[4,4,96,3072]{3,2,1,0:T(8,128)(2,1)} %bitcast.4), custom_call_target="tpu_custom_call" | custom-call | tf_op jit(solution)/shard_map/reduce_shares/pallas_call | solution.py:237
  530.3 2.4 broadcast_multiply_fusion
  (2 shorter events, 0.0 us)
Async XLA Ops:
  6.3 19.9 %all-to-all-start.1 = ((f32[16,2,296]{2,1,0:T(2,128)}), f32[16,2,296]{2,1,0:T(2,128)S(1)}, u32[]{:S(2)}, u32[]{:S(2)}) async-start(f32[16,2,296]{2,1,0:T(2,128)} %pack_meta.1), calls=%async_computation.1 | async-start | bytes 98304 | tf_op jit(solution)/shard_map/all_to_all | solution.py:280
  26.2 279.7 %all-to-all-start = ((bf16[16,296,1536]{2,1,0:T(8,128)(2,1)}), bf16[16,296,1536]{2,1,0:T(8,128)(2,1)}, u32[]{:S(2)}, u32[]{:S(2)}) async-start(bf16[16,296,1536]{2,1,0:T(8,128)(2,1)} %pack.1), calls=%async_computation | async-start | bytes 29097984 | tf_op jit(solution)/shard_map/all_to_all | solution.py:288
  305.9 24.8 %copy-start = (f32[1024]{0:T(1024)S(1)}, f32[1024]{0:T(1024)}, u32[]{:S(2)}) copy-start(f32[1024]{0:T(1024)} %param.9) | copy-start | bytes 12292
  305.9 24.8 %copy-start.1 = (f32[1024]{0:T(1024)S(1)}, f32[1024]{0:T(1024)}, u32[]{:S(2)}) copy-start(f32[1024]{0:T(1024)} %param.8) | copy-start | bytes 12292
  330.7 5.9 %collective-permute-start = (bf16[1024,1536]{1,0:T(8,128)(2,1)}, bf16[1024,1536]{1,0:T(8,128)(2,1)S(1)}, u32[]{:S(2)}, u32[]{:S(2)}) collective-permute-start(bf16[1024,1536]{1,0:T(8,128)(2,1)} %histogram.3), channel_id=1, source_target_pairs={{0,1},{1,0},{2,3},{3,2},{4,5},{5,4},{6,7},{7,6},{8,9},{9,8},{10,11... | collective-permute-start | bytes 9437192 | tf_op jit(solution)/shard_map/ppermute | solution.py:18
